TPU v7x, 512 devices: a whole 4x8x8 slice. The times are simulated.
512 devices in a mesh: sub: 128 (over y, z, core), pln: 4 (over x).
Axes of the slice: x: 4, y: 8, z: 8, core: 2. Of those that a mesh axis runs over, the one named last changes fastest.
Arguments:
- labels: int32 [8, 64, 16384], P('pln', None, 'sub'), may hold values from 0 to 3
- levels: float32 [4], replicated, may hold values from 0.1 to 1
- zvec: bfloat16 [64, 8, 64, 16384], P(None, 'pln', None, 'sub'), may hold values from -1 to 1
- resid: float32 [8, 64, 16384], P('pln', None, 'sub'), may hold values from -6 to 6
Outputs:
- coarse_solution: float32 [128, 64], P('sub')
- deflated: float32 [8, 64, 16384], P('pln', None, 'sub')
All inputs are finite; a program needn't handle non-finite values.
Results may differ from a plain program's by a relative error of at most 0.0003.
Values may be sent and summed in bfloat16 or wider, within the bound.
A program may use at most 128 MiB of HBM per device.

v0:
```python
import jax
import jax.numpy as jnp
from jax import lax
from jax.sharding import PartitionSpec as P

CITERS = 2


PRECISE = lax.Precision.HIGHEST


def from_behind(value, axis, by):
    devices = lax.axis_size(axis)
    return lax.ppermute(value, axis, [(i, (i + by) % devices) for i in range(devices)])


def with_halo(block, sides, width, periodic):
    for axis, dim in sides:
        count = lax.axis_size(axis)
        forward = [(i, i + 1) for i in range(count - 1)]
        if periodic:
            forward.append((count - 1, 0))
        backward = [(target, source) for source, target in forward]
        low = lax.ppermute(
            lax.slice_in_dim(block, block.shape[dim] - width, None, axis=dim), axis, forward
        )
        high = lax.ppermute(lax.slice_in_dim(block, 0, width, axis=dim), axis, backward)
        block = jnp.concatenate([low, block, high], axis=dim)
    return block


def harmonic(left_value, right_value):
    return 2.0 * left_value * right_value / (left_value + right_value)


def coefficients(labels, levels):
    weighted = jnp.zeros(labels.shape, jnp.float32)
    for level_index in range(levels.shape[0]):
        weighted = weighted + jnp.where(labels == level_index, levels[level_index], 0.0)
    return weighted


def apply_yz(fine_field, weights, z_below, z_above):
    zero_plane = jnp.zeros_like(fine_field[..., :1, :])
    below_y = jnp.concatenate([zero_plane, fine_field[..., :-1, :]], axis=-2)
    above_y = jnp.concatenate([fine_field[..., 1:, :], zero_plane], axis=-2)
    below_z = jnp.concatenate([z_below, fine_field[..., :-1]], axis=-1)
    above_z = jnp.concatenate([fine_field[..., 1:], z_above], axis=-1)
    return (
        weights[2] * (fine_field - below_y)
        + weights[3] * (fine_field - above_y)
        + weights[4] * (fine_field - below_z)
        + weights[5] * (fine_field - above_z)
    )


def apply_full(fine_field, weights, x_below, x_above, z_below, z_above):
    below_x = jnp.concatenate([x_below, fine_field[..., :-1, :, :]], axis=-3)
    above_x = jnp.concatenate([fine_field[..., 1:, :, :], x_above], axis=-3)
    return (
        weights[0] * (fine_field - below_x)
        + weights[1] * (fine_field - above_x)
        + apply_yz(fine_field, weights, z_below, z_above)
    )


def coarse_apply(diag_block, upper_block, direction):
    ahead_term = from_behind(direction, "sub", -1)
    behind_term = from_behind(jnp.dot(direction, upper_block, precision=PRECISE), "sub", 1)
    return (
        jnp.dot(diag_block, direction, precision=PRECISE)
        + jnp.dot(upper_block, ahead_term, precision=PRECISE)
        + behind_term
    )


def residual_norm(remain):
    return lax.psum(jnp.dot(remain, remain, precision=PRECISE), "sub")


def body(labels, levels, zvec, resid):
    first_pln = lax.axis_index("pln") == 0
    last_pln = lax.axis_index("pln") == lax.axis_size("pln") - 1
    density_coef = coefficients(labels, levels)
    padded = with_halo(density_coef.astype(jnp.bfloat16), (("pln", 0), ("sub", 2)), 1, True).astype(
        density_coef.dtype
    )
    lower_plane = jnp.where(first_pln, density_coef[:1], padded[:1, :, 1:-1])
    upper_plane = jnp.where(last_pln, density_coef[-1:], padded[-1:, :, 1:-1])
    below_x = jnp.concatenate([lower_plane, density_coef[:-1]], axis=0)
    above_x = jnp.concatenate([density_coef[1:], upper_plane], axis=0)
    pad_y = jnp.pad(density_coef, ((0, 0), (1, 1), (0, 0)), mode="edge")
    weights = (
        harmonic(density_coef, below_x),
        harmonic(density_coef, above_x),
        harmonic(density_coef, pad_y[:, :-2]),
        harmonic(density_coef, pad_y[:, 2:]),
        harmonic(density_coef, padded[1:-1, :, :-2]),
        harmonic(density_coef, padded[1:-1, :, 2:]),
    )
    mode_count = zvec.shape[0]
    modes_wide = zvec.astype(jnp.float32)
    flat_modes = modes_wide.reshape(mode_count, -1)
    z_zero = jnp.zeros_like(modes_wide[..., :1])
    modes_pad = with_halo(zvec, (("pln", 1),), 1, False)
    stencil_image = apply_full(
        modes_wide,
        weights,
        modes_pad[:, :1].astype(jnp.float32),
        modes_pad[:, -1:].astype(jnp.float32),
        z_zero,
        z_zero,
    )
    diag_block = jnp.dot(flat_modes, stencil_image.reshape(mode_count, -1).T, precision=PRECISE)
    next_first = from_behind(zvec[..., :1], "sub", -1)
    edge_rows = (modes_wide[..., -1] * weights[5][..., -1]).reshape(mode_count, -1)
    upper_block = -jnp.dot(
        edge_rows, next_first.astype(jnp.float32).reshape(mode_count, -1).T, precision=PRECISE
    )
    coarse_rhs = jnp.dot(flat_modes, resid.reshape(-1), precision=PRECISE)
    diag_block, upper_block, coarse_rhs = lax.psum((diag_block, upper_block, coarse_rhs), "pln")
    solution = jnp.zeros_like(coarse_rhs)
    remain = coarse_rhs
    direction = coarse_rhs
    norm_now = residual_norm(remain)
    for iteration in range(CITERS):
        stencil_image = coarse_apply(diag_block, upper_block, direction)
        step_size = norm_now / lax.psum(jnp.dot(direction, stencil_image, precision=PRECISE), "sub")
        solution = solution + step_size * direction
        remain = remain - step_size * stencil_image
        if iteration + 1 < CITERS:
            norm_next = residual_norm(remain)
            direction = remain + norm_next / norm_now * direction
            norm_now = norm_next
    fine_field = jnp.dot(solution, flat_modes, precision=PRECISE).reshape(resid.shape)
    field_pad = with_halo(
        fine_field.astype(jnp.bfloat16), (("pln", 0), ("sub", 2)), 1, True
    ).astype(fine_field.dtype)
    x_below = jnp.where(first_pln, 0.0, field_pad[:1, :, 1:-1])
    x_above = jnp.where(last_pln, 0.0, field_pad[-1:, :, 1:-1])
    stencil_image = apply_full(
        fine_field, weights, x_below, x_above, field_pad[1:-1, :, :1], field_pad[1:-1, :, -1:]
    )
    return (solution[None], resid - stencil_image)


def solution(mesh):
    in_specs = (P("pln", None, "sub"), P(), P(None, "pln", None, "sub"), P("pln", None, "sub"))
    out_specs = (P("sub", None), P("pln", None, "sub"))
    return jax.shard_map(body, mesh=mesh, in_specs=in_specs, out_specs=out_specs, check_vma=False)
```

profile of v0, /device:TPU:1, one launch (start us, length us, event | category | flops | bytes accessed | tf_op | source)
XLA Modules:
  0.0 894.3 jit_solution(11589215300036182164)
XLA Ops:
  2.1 3.3 fusion.61
  5.5 3.9 collective-permute-start
  9.4 3.2 collective-permute-start.1
  12.6 3.1 fusion.65
  15.7 3.1 collective-permute-start.4
  21.7 7.9 collective-permute-start.6
  29.6 5.0 fusion.62
  34.7 4.1 fusion.63
  38.8 2.5 fusion.64
  41.3 3.2 fusion.30
  46.6 8.2 collective-permute-start.3
  59.5 5.3 slice_multiply_fusion
  64.9 3.6 copy.35
  72.0 7.1 fusion.2
  79.1 5.5 fusion.20
  84.6 14.0 %all-reduce.7 = (f32[64]{0:T(128)S(1)}, f32[64,64]{1,0:T(8,128)S(1)}, f32[64,64]{0,1:T(8,128)S(1)}) all-reduce(f32[64]{0:T(128)S(1)} %fusion.30, f32[64,64]{1,0:T(8,128)S(1)} %fusion.19, f32[64,64]{0,1:T(8,128)S(1)} %fusion.20), channel_id=1, replica_groups=mesh['sub'=128,'pln'=4] {'pln'}, use_global_device_ids=true, to_apply=%region_0.1 | all-reduce | flops 8256 | bytes 66048 | tf_op jit(solution)/shard_map/psum | solution.py:121
  98.6 10.7 %collective-permute-start.7 = (f32[64]{0:T(128)S(1)}, f32[64]{0:T(128)S(1)}, u32[]{:S(2)}, u32[]{:S(2)}) collective-permute-start(f32[64]{0:T(128)S(1)} %get-tuple-element.6), channel_id=1, source_target_pairs={{0,508},{4,0},{8,4},{12,8},{16,12},{20,16},{24,20},{28,24},{32,28}... | collective-permute-start | bytes 776 | tf_op jit(solution)/shard_map/ppermute | solution.py:14
  113.4 252.4 %all-reduce.6 = (f32[]{:T(128)}, f32[]{:T(128)}) all-reduce(f32[]{:T(128)} %get-tuple-element.3, f32[]{:T(128)} %get-tuple-element.2), channel_id=1, replica_groups=mesh['sub'=128,'pln'=4] {'sub'}, use_global_device_ids=true, to_apply=%region_1.2 | all-reduce | flops 2 | bytes 16 | tf_op jit(solution)/shard_map/psum | solution.py:78
  367.8 247.4 %psum.54 = f32[]{:T(128)} all-reduce(f32[]{:T(128)} %multiply_reduce_fusion), channel_id=1, replica_groups=mesh['sub'=128,'pln'=4] {'sub'}, use_global_device_ids=true, to_apply=%region_5.6 | all-reduce | flops 1 | bytes 8 | tf_op jit(solution)/shard_map/psum | solution.py:78
  616.7 2.6 collective-permute-start.9
  619.3 3.0 collective-permute-start.10
  623.8 251.5 %psum.55 = f32[]{:T(128)} all-reduce(f32[]{:T(128)} %fusion.33), channel_id=1, replica_groups=mesh['sub'=128,'pln'=4] {'sub'}, use_global_device_ids=true, to_apply=%region_6.7 | all-reduce | flops 1 | bytes 8 | tf_op jit(solution)/shard_map/psum | solution.py:128
  880.4 4.6 collective-permute-start.12
  887.8 3.7 collective-permute-start.14
  (75 shorter events, 30.4 us)
Async XLA Ops:
  0.6 19.4 %copy-start = (bf16[64,2,64,128]{3,2,1,0:T(8,128)(2,1)S(1)}, bf16[64,2,64,128]{3,2,1,0:T(8,128)(2,1)}, u32[]{:S(2)}) copy-start(bf16[64,2,64,128]{3,2,1,0:T(8,128)(2,1)} %param.6) | copy-start | bytes 6291460
  5.5 39.0 %collective-permute-start = (bf16[1,64,128]{2,1,0:T(8,128)(2,1)S(1)}, bf16[1,64,128]{2,1,0:T(8,128)(2,1)S(1)}, u32[]{:S(2)}, u32[]{:S(2)}) collective-permute-start(bf16[1,64,128]{2,1,0:T(8,128)(2,1)S(1)} %get-tuple-element.47), channel_id=1, source_target_pairs={{0,1},{1,2},{2,3},{3,0},{4,5},{5,6},{6,7},{7,4},{8,9},{9,10},{10,1... | collective-permute-start | bytes 49160 | tf_op jit(solution)/shard_map/ppermute | solution.py:24
  9.4 35.1 %collective-permute-start.1 = (bf16[1,64,128]{2,1,0:T(8,128)(2,1)S(1)}, bf16[1,64,128]{2,1,0:T(8,128)(2,1)S(1)}, u32[]{:S(2)}, u32[]{:S(2)}) collective-permute-start(bf16[1,64,128]{2,1,0:T(8,128)(2,1)S(1)} %get-tuple-element.48), channel_id=1, source_target_pairs={{1,0},{2,1},{3,2},{0,3},{5,4},{6,5},{7,6},{4,7},{9,8},{10,9},{11,1... | collective-permute-start | bytes 49160 | tf_op jit(solution)/shard_map/ppermute | solution.py:27
  15.7 54.0 %collective-permute-start.4 = (bf16[64,1,64,128]{3,2,1,0:T(8,128)(2,1)}, bf16[64,1,64,128]{3,2,1,0:T(8,128)(2,1)}, u32[]{:S(2)}, u32[]{:S(2)}) collective-permute-start(bf16[64,1,64,128]{3,2,1,0:T(8,128)(2,1)} %get-tuple-element.18), channel_id=1, source_target_pairs={{0,1},{1,2},{2,3},{4,5},{5,6},{6,7},{8,9},{9,10},{10,11},{12,13},{... | collective-permute-start | bytes 3145736 | tf_op jit(solution)/shard_map/ppermute | solution.py:24
  18.8 53.0 %collective-permute-start.5 = (bf16[64,1,64,128]{3,2,1,0:T(8,128)(2,1)}, bf16[64,1,64,128]{3,2,1,0:T(8,128)(2,1)S(1)}, u32[]{:S(2)}, u32[]{:S(2)}) collective-permute-start(bf16[64,1,64,128]{3,2,1,0:T(8,128)(2,1)} %get-tuple-element.17), channel_id=1, source_target_pairs={{1,0},{2,1},{3,2},{5,4},{6,5},{7,6},{9,8},{10,9},{11,10},{13,12},{... | collective-permute-start | bytes 3145736 | tf_op jit(solution)/shard_map/ppermute | solution.py:27
  21.7 46.7 %collective-permute-start.6 = (bf16[64,2,64,1]{2,0,1,3:T(8,128)(2,1)}, bf16[64,2,64,1]{2,0,1,3:T(8,128)(2,1)}, u32[]{:S(2)}, u32[]{:S(2)}) collective-permute-start(bf16[64,2,64,1]{2,0,1,3:T(8,128)(2,1)} %copy.53), channel_id=1, source_target_pairs={{0,508},{4,0},{8,4},{12,8},{16,12},{20,16},{24,20},{28,24},{32,28}... | collective-permute-start | bytes 49160 | tf_op jit(solution)/shard_map/ppermute | solution.py:14
  38.8 2.5 copy-start.8
  44.6 12.5 %collective-permute-start.2 = (bf16[4,64,1]{2,1,0:T(8,128)(2,1)S(1)}, bf16[4,64,1]{2,1,0:T(8,128)(2,1)S(1)}, u32[]{:S(2)}, u32[]{:S(2)}) collective-permute-start(bf16[4,64,1]{2,1,0:T(8,128)(2,1)S(1)} %get-tuple-element.43), channel_id=1, source_target_pairs={{0,4},{4,8},{8,12},{12,16},{16,20},{20,24},{24,28},{28,32},{32,36}... | collective-permute-start | bytes 1544 | tf_op jit(solution)/shard_map/ppermute | solution.py:24
  46.6 10.6 %collective-permute-start.3 = (bf16[4,64,1]{2,1,0:T(8,128)(2,1)S(1)}, bf16[4,64,1]{2,1,0:T(8,128)(2,1)S(1)}, u32[]{:S(2)}, u32[]{:S(2)}) collective-permute-start(bf16[4,64,1]{2,1,0:T(8,128)(2,1)S(1)} %get-tuple-element.44), channel_id=1, source_target_pairs={{4,0},{8,4},{12,8},{16,12},{20,16},{24,20},{28,24},{32,28},{36,32}... | collective-permute-start | bytes 1544 | tf_op jit(solution)/shard_map/ppermute | solution.py:27
  68.4 3.5 copy-start.1
  68.4 3.5 copy-start.2
  68.5 3.6 copy-start.3
  68.5 3.6 copy-start.4
  79.1 814.5 %copy-start.5 = (f32[2,64,128]{2,1,0:T(8,128)S(1)}, f32[2,64,128]{2,1,0:T(8,128)}, u32[]{:S(2)}) copy-start(f32[2,64,128]{2,1,0:T(8,128)} %get-tuple-element.42) | copy-start | bytes 196612
  79.1 814.5 %copy-start.9 = (f32[2,64,128]{2,1,0:T(8,128)S(1)}, f32[2,64,128]{2,1,0:T(8,128)}, u32[]{:S(2)}) copy-start(f32[2,64,128]{2,1,0:T(8,128)} %param.7) | copy-start | bytes 196612
  98.6 14.0 %collective-permute-start.7 = (f32[64]{0:T(128)S(1)}, f32[64]{0:T(128)S(1)}, u32[]{:S(2)}, u32[]{:S(2)}) collective-permute-start(f32[64]{0:T(128)S(1)} %get-tuple-element.6), channel_id=1, source_target_pairs={{0,508},{4,0},{8,4},{12,8},{16,12},{20,16},{24,20},{28,24},{32,28}... | collective-permute-start | bytes 776 | tf_op jit(solution)/shard_map/ppermute | solution.py:14
  109.5 3.1 collective-permute-start.8
  616.7 6.3 collective-permute-start.9
  619.3 3.7 collective-permute-start.10
  876.6 17.7 %copy-start.10 = (f32[64]{0:T(128)}, f32[64]{0:T(128)S(1)}, u32[]{:S(2)}) copy-start(f32[64]{0:T(128)S(1)} %multiply_add_fusion) | copy-start | bytes 772
  878.5 6.6 collective-permute-start.11
  880.4 5.4 collective-permute-start.12
  885.9 5.6 collective-permute-start.13
  887.8 5.6 collective-permute-start.14
  (2 other events, 1.3 us)
where the time goes:
time: 899 us; the launch traced here: 894 us
  blocking collectives  765 us (85%)
  starting transfers between devices  59.8 us (7%)
  other arithmetic  23.6 us (3%)
  local copies, waits for them, and re-layouts  22.5 us (3%)
  matrix products  13.8 us (2%)
    psum x2, blocking collectives, residual_norm(): return lax.psum(jnp.dot(remain, remain, precision=PRECISE), 'sub')  500 us
    psum x1, blocking collectives, body(): lax.psum(jnp.dot(direction, stencil_image, precision=PRECISE), 'sub')  251 us
    ppermute x5, starting transfers between devices, from_behind(): lax.ppermute(value, axis, [(i, (i + by) % devices) for i in range(devices)])  26.1 us
    ppermute x5, starting transfers between devices, with_halo(): lax.ppermute(lax.slice_in_dim(block, 0, width, axis=dim), axis, backward)  20.9 us
  transfers between devices with their start and end apart: 15, of which 4 were waited for; matrix products, arithmetic and copies ran while one was open for 4% of the time, Pallas kernels for 0%

commit v1 on v0

v1 whole, which is shorter than its diff:
```python
import functools
import math

import jax
import jax.numpy as jnp
from jax import lax
from jax.experimental import pallas as pl
from jax.experimental.pallas import tpu as pltpu
from jax.sharding import PartitionSpec as P

MESH = pl.DeviceIdType.MESH
PRECISE = lax.Precision.HIGHEST
ZCHUNKS = 4
STEP = 4


def harmonic(left_value, right_value):
    return 2.0 * left_value * right_value / (left_value + right_value)


def kernel(
    sides,
    levels,
    labels_hbm,
    z_hbm,
    resid_hbm,
    sol_ref,
    defl_ref,
    z,
    lab,
    res,
    lab_x,
    lab_z,
    field,
    field_x,
    field_z,
    spread,
    part,
    rows,
    sums,
    wts,
    load_sem,
    side_send,
    side_recv,
    row_send,
    row_recv,
    sum_send,
    sum_recv,
):
    ny, nz, npln = sides
    nsub = ny * nz * 2
    modes, planes, height, depth = z.shape
    sub = lax.axis_index("sub")
    pln = lax.axis_index("pln")
    core = sub % 2
    zc = (sub // 2) % nz
    yc = sub // (2 * nz)
    first_pln = pln == 0
    last_pln = pln == npln - 1

    per = modes // ZCHUNKS
    small = (
        pltpu.make_async_copy(labels_hbm, lab, load_sem.at[0]),
        pltpu.make_async_copy(resid_hbm, res, load_sem.at[1]),
    )
    big = [
        pltpu.make_async_copy(
            z_hbm.at[pl.ds(i * per, per)], z.at[pl.ds(i * per, per)], load_sem.at[2 + i]
        )
        for i in range(ZCHUNKS)
    ]
    for copy in small:
        copy.start()
    for copy in big:
        copy.start()

    def group(stage):
        if stage == 0:
            count, me = npln * 2, pln * 2 + core
        elif stage == 1:
            count, me = nz, zc
        else:
            count, me = ny, yc
        peers = []
        for off in range(1, count):
            other = (me + off) % count
            if stage == 0:
                peers.append((sub - core + other % 2, other // 2))
            elif stage == 1:
                peers.append(((yc * nz + other) * 2 + core, pln))
            else:
                peers.append(((other * nz + zc) * 2 + core, pln))
        return count, me, peers

    groups = [group(stage) for stage in range(3)]
    ahead = ((sub + 1) % nsub, pln)
    behind = ((sub + nsub - 1) % nsub, pln)
    right = (sub, (pln + 1) % npln)
    left = (sub, (pln + npln - 1) % npln)
    far = ((sub + 2 * core + nsub - 1) % nsub, pln)

    barrier = pltpu.get_barrier_semaphore()
    total = 1
    pl.semaphore_signal(barrier, inc=1, device_id=far, device_id_type=MESH)
    for _, _, peers in groups:
        for peer in peers:
            pl.semaphore_signal(barrier, inc=1, device_id=peer, device_id_type=MESH)
            total += 1
    pl.semaphore_wait(barrier, total)

    pending = []

    def side_copies(which, src, dst_x, dst_z):
        copies = []
        for side, (piece, target, place) in enumerate(
            (
                (src.at[planes - 1], right, dst_x.at[0]),
                (src.at[0], left, dst_x.at[1]),
                (src, ahead, dst_z.at[0]),
                (src, behind, dst_z.at[1]),
            )
        ):
            copies.append(
                pltpu.make_async_remote_copy(
                    src_ref=piece,
                    dst_ref=place,
                    send_sem=side_send.at[which, side],
                    recv_sem=side_recv.at[which, side],
                    device_id=target,
                    device_id_type=MESH,
                )
            )
        pending.extend(copies)
        return copies

    def rows_send(which, row):
        rows[which, pln] = row
        for off in range(1, npln):
            copy = pltpu.make_async_remote_copy(
                src_ref=rows.at[which, pln],
                dst_ref=rows.at[which, pln],
                send_sem=row_send.at[which],
                recv_sem=row_recv.at[which],
                device_id=(sub, (pln + off) % npln),
                device_id_type=MESH,
            )
            copy.start()

    def rows_wait(which):
        both = rows.at[which, pl.ds(0, npln - 1)]
        pltpu.make_async_copy(both, both, row_recv.at[which]).wait()
        result = rows[which, 0]
        for i in range(1, npln):
            result = result + rows[which, i]
        return result

    def sums_send(which, stage, row):
        count, me, peers = groups[stage]
        sums[which, stage, me] = row
        for peer in peers:
            copy = pltpu.make_async_remote_copy(
                src_ref=sums.at[which, stage, me],
                dst_ref=sums.at[which, stage, me],
                send_sem=sum_send.at[which, stage],
                recv_sem=sum_recv.at[which, stage],
                device_id=peer,
                device_id_type=MESH,
            )
            copy.start()

    def sums_wait(which, stage):
        count, _, _ = groups[stage]
        both = sums.at[which, stage, pl.ds(0, count - 1)]
        pltpu.make_async_copy(both, both, sum_recv.at[which, stage]).wait()
        result = sums[which, stage, 0]
        for i in range(1, count):
            result = result + sums[which, stage, i]
        return result

    lane = lax.broadcasted_iota(jnp.int32, (1, depth), 1)

    def whole(value):
        if value.ndim == 3:
            value = jnp.sum(value.reshape(-1, 8, value.shape[-1]), axis=0)
        return jnp.sum(jnp.sum(value, axis=0, keepdims=True), axis=1, keepdims=True)

    def packet(*values):
        row = jnp.zeros((1, depth), jnp.float32)
        for i, value in enumerate(values):
            row = jnp.where(lane == i, value, row)
        return row

    def entry(row, i):
        return jnp.sum(jnp.where(lane == i, row, 0.0), axis=1, keepdims=True)

    def project_some(value, start, stop):
        @pl.loop(start // STEP, stop // STEP)
        def _(block):
            for inner in range(STEP):
                k = block * STEP + inner
                product = z[k].astype(jnp.float32) * value
                slim = jnp.sum(product.reshape(-1, 8, depth), axis=0)
                part[pl.ds(k, 1), :] = jnp.sum(slim, axis=0, keepdims=True)

    def project_row():
        ones = jnp.ones((8, depth), jnp.float32)
        gathered = lax.dot_general(
            ones, part[...], (((1,), (1,)), ((), ())), precision=PRECISE,
            preferred_element_type=jnp.float32,
        )
        row = gathered[:1]
        return jnp.concatenate([row, jnp.zeros((1, depth - modes), jnp.float32)], axis=1)

    def spread_row(row):
        here = lax.broadcasted_iota(jnp.int32, (modes, depth), 0)
        there = lax.broadcasted_iota(jnp.int32, (modes, depth), 1)
        picked = jnp.where(here == there, jnp.broadcast_to(row, (modes, depth)), 0.0)
        spread[...] = jnp.broadcast_to(jnp.sum(picked, axis=1, keepdims=True), (modes, depth))

    def expand_plane(plane):
        def some(block, acc):
            for inner in range(STEP):
                k = block * STEP + inner
                scale = jnp.broadcast_to(spread[pl.ds(k, 1), :], (height, depth))
                acc = acc + z[k, plane].astype(jnp.float32) * scale
            return acc

        return lax.fori_loop(0, modes // STEP, some, jnp.zeros((height, depth), jnp.float32))

    y_index = lax.broadcasted_iota(jnp.int32, (planes, height, depth), 1)
    z_index = lax.broadcasted_iota(jnp.int32, (planes, height, depth), 2)

    def along_z(value, before, after):
        low = jnp.where(z_index == 0, pltpu.roll(before, 1, 2), pltpu.roll(value, 1, 2))
        high = jnp.where(
            z_index == depth - 1,
            pltpu.roll(after, depth - 1, 2),
            pltpu.roll(value, depth - 1, 2),
        )
        return low, high

    def stencil(which):
        value = field[which]
        zero = jnp.zeros_like(value)
        x_low = jnp.where(first_pln, 0.0, field_x[which, 0])
        x_high = jnp.where(last_pln, 0.0, field_x[which, 1])
        x_below = jnp.concatenate([x_low[None], value[:-1]], axis=0)
        x_above = jnp.concatenate([value[1:], x_high[None]], axis=0)
        y_below = jnp.where(y_index == 0, zero, pltpu.roll(value, 1, 1))
        y_above = jnp.where(y_index == height - 1, zero, pltpu.roll(value, height - 1, 1))
        z_below, z_above = along_z(value, field_z[which, 0], field_z[which, 1])
        return (
            wts[0] * (value - x_below)
            + wts[1] * (value - x_above)
            + wts[2] * (value - y_below)
            + wts[3] * (value - y_above)
            + wts[4] * (value - z_below)
            + wts[5] * (value - z_above)
        )

    small[0].wait()
    label_copies = side_copies(0, lab, lab_x, lab_z)
    for copy in label_copies:
        copy.start()

    small[1].wait()
    for i in range(ZCHUNKS):
        big[i].wait()
        project_some(res[...], i * per, (i + 1) * per)
    rows_send(0, project_row())

    def density(labels):
        value = jnp.full(labels.shape, levels[0], jnp.float32)
        for i in range(1, levels.shape[0]):
            value = jnp.where(labels == i, levels[i], value)
        return value

    for copy in label_copies:
        copy.wait_recv()
    coef = density(lab[...])
    low = jnp.where(first_pln, coef[0], density(lab_x[0]))
    high = jnp.where(last_pln, coef[planes - 1], density(lab_x[1]))
    wts[0] = harmonic(coef, jnp.concatenate([low[None], coef[:-1]], axis=0))
    wts[1] = harmonic(coef, jnp.concatenate([coef[1:], high[None]], axis=0))
    wts[2] = harmonic(coef, jnp.where(y_index == 0, coef, pltpu.roll(coef, 1, 1)))
    wts[3] = harmonic(
        coef, jnp.where(y_index == height - 1, coef, pltpu.roll(coef, height - 1, 1))
    )
    z_low, z_high = along_z(coef, density(lab_z[0]), density(lab_z[1]))
    wts[4] = harmonic(coef, z_low)
    wts[5] = harmonic(coef, z_high)

    def expand(which):
        copies = side_copies(which + 1, field.at[which], field_x.at[which], field_z.at[which])
        for plane in range(planes):
            field[which, plane] = expand_plane(plane)
            if plane == 0:
                copies[1].start()
        copies[0].start()
        copies[2].start()
        copies[3].start()
        return copies

    share = 1.0 / npln
    rhs = rows_wait(0)
    spread_row(rhs)
    copies = expand(0)
    norm_part = jnp.sum(rhs * rhs, axis=1, keepdims=True) * share
    for copy in copies:
        copy.wait_recv()
    image = stencil(0)
    sums_send(0, 0, packet(norm_part, whole(field[0] * image)))
    project_some(image, 0, modes)
    rows_send(1, project_row())
    sums_send(0, 1, sums_wait(0, 0))

    image_row = rows_wait(1)
    spread_row(image_row)
    copies = expand(1)
    sums_send(0, 2, sums_wait(0, 1))
    for copy in copies:
        copy.wait_recv()
    image_next = stencil(1)
    firsts = sums_wait(0, 2)
    norm = entry(firsts, 0)
    curve = entry(firsts, 1)
    alpha = norm / curve
    remain = rhs - alpha * image_row
    remain_field = field[0] - alpha[:, :, None] * field[1]
    remain_image = image - alpha[:, :, None] * image_next
    sums_send(
        1,
        0,
        packet(
            jnp.sum(remain * remain, axis=1, keepdims=True) * share,
            jnp.sum(remain * image_row, axis=1, keepdims=True) * share,
            whole(remain_field * remain_image),
        ),
    )
    sums_send(1, 1, sums_wait(1, 0))
    sums_send(1, 2, sums_wait(1, 1))
    seconds = sums_wait(1, 2)
    norm_next = entry(seconds, 0)
    beta = norm_next / norm
    curve_next = entry(seconds, 2) + 2.0 * beta * entry(seconds, 1) + beta * beta * curve
    alpha_next = norm_next / curve_next
    solution_row = alpha * rhs + alpha_next * (remain + beta * rhs)
    sol_ref[...] = solution_row[:, :modes]
    first_part = (alpha + alpha_next * beta)[:, :, None]
    defl_ref[...] = res[...] - first_part * image - alpha_next[:, :, None] * remain_image

    for copy in pending:
        copy.wait_send()
    for which in range(2):
        both = rows.at[which, pl.ds(0, npln - 1)]
        pltpu.make_async_copy(both, both, row_send.at[which]).wait()
        for stage, (count, _, _) in enumerate(groups):
            both = sums.at[which, stage, pl.ds(0, count - 1)]
            pltpu.make_async_copy(both, both, sum_send.at[which, stage]).wait()


def body(sides, labels, levels, zvec, resid):
    modes = zvec.shape[0]
    block = resid.shape
    ny, nz, npln = sides
    widest = max(npln * 2, nz, ny)
    lanes = block[-1]
    anywhere = pl.BlockSpec(memory_space=pltpu.HBM)
    vmem = pl.BlockSpec(memory_space=pltpu.VMEM)
    dma = pltpu.SemaphoreType.DMA
    return pl.pallas_call(
        functools.partial(kernel, sides),
        out_shape=(
            jax.ShapeDtypeStruct((1, modes), jnp.float32),
            jax.ShapeDtypeStruct(block, jnp.float32),
        ),
        in_specs=[pl.BlockSpec(memory_space=pltpu.SMEM), anywhere, anywhere, anywhere],
        out_specs=(vmem, vmem),
        scratch_shapes=[
            pltpu.VMEM(zvec.shape, zvec.dtype),
            pltpu.VMEM(block, labels.dtype),
            pltpu.VMEM(block, jnp.float32),
            pltpu.VMEM((2,) + block[1:], labels.dtype),
            pltpu.VMEM((2,) + block, labels.dtype),
            pltpu.VMEM((2,) + block, jnp.float32),
            pltpu.VMEM((2, 2) + block[1:], jnp.float32),
            pltpu.VMEM((2, 2) + block, jnp.float32),
            pltpu.VMEM((modes, lanes), jnp.float32),
            pltpu.VMEM((modes, lanes), jnp.float32),
            pltpu.VMEM((2, npln, 1, lanes), jnp.float32),
            pltpu.VMEM((2, 3, widest, 1, lanes), jnp.float32),
            pltpu.VMEM((6,) + block, jnp.float32),
            dma((2 + ZCHUNKS,)),
            dma((3, 4)),
            dma((3, 4)),
            dma((2,)),
            dma((2,)),
            dma((2, 3)),
            dma((2, 3)),
        ],
        compiler_params=pltpu.CompilerParams(
            collective_id=0, has_side_effects=True, vmem_limit_bytes=63 << 20
        ),
        name="deflated_coarse",
    )(levels, labels, zvec, resid)


def solution(mesh):
    chips = mesh.shape["sub"] // 2
    side = math.isqrt(chips)
    sides = (chips // side, side, mesh.shape["pln"])
    in_specs = (P("pln", None, "sub"), P(), P(None, "pln", None, "sub"), P("pln", None, "sub"))
    out_specs = (P("sub", None), P("pln", None, "sub"))
    return jax.shard_map(
        functools.partial(body, sides), mesh=mesh, in_specs=in_specs, out_specs=out_specs,
        check_vma=False,
    )
```

time: 899 us -> 52.6 us (0.06)
  blocking collectives: 765 us -> 0 us
  starting transfers between devices: 59.8 us -> 0 us
  Pallas kernels: 0 us -> 48.6 us
  other arithmetic: 23.6 us -> 0 us
  local copies, waits for them, and re-layouts: 22.5 us -> 2.59 us
  matrix products: 13.8 us -> 0 us
    psum x4 -> x0, blocking collectives: 765 us -> none  [the longest x2 500 us: residual_norm(): return lax.psum(jnp.dot(remain, remain, precision=PRECISE), 'sub')]
    ppermute x15 -> x0, starting transfers between devices: 59.8 us -> none  [the longest x5 26.1 us: from_behind(): lax.ppermute(value, axis, [(i, (i + by) % devices) for i in range(devices)])]
    pallas_call x0 -> x1, Pallas kernels: none -> 48.6 us  [body(): pl.pallas_call(functools.partial(kernel, sides), out_shape=(jax.ShapeDtyp...]
    slice x14 -> x0, local copies, waits for them, and re-layouts: 16.7 us -> none  [the longest x2 5.06 us: apply_yz(): below_y = jnp.concatenate([zero_plane, fine_field[..., :-1, :]], axis=-2)]
    dot_general x10 -> x0, matrix products: 13.8 us -> none  [the longest x1 5.49 us: body(): jnp.dot(flat_modes, stencil_image.reshape(mode_count, -1).T, precision=PR...]
  transfers between devices with their start and end apart: 15 -> 0, of which waited for: 4 -> 0; matrix products, arithmetic and copies ran while one was open for 4% -> 0% of each run, Pallas kernels for 0% -> 0%
where the time goes in v1:
time: 52.6 us; the launch traced here: 51.8 us
  Pallas kernels  48.6 us (92%)
  local copies, waits for them, and re-layouts  2.59 us (5%)
  between operations  0.64 us (1%)
    pallas_call x1, Pallas kernels, body(): pl.pallas_call(functools.partial(kernel, sides), out_shape=(jax.ShapeDtyp...  48.6 us
    unnamed x2, local copies, waits for them, and re-layouts  2.59 us

profile of v1, /device:TPU:1, one launch (start us, length us, event | category | flops | bytes accessed | tf_op | source)
XLA Modules:
  0.0 51.8 jit_solution(593681777037142348)
XLA Ops:
  0.6 48.6 %deflated_coarse.1 = (f32[1,64]{1,0:T(1,128)}, f32[2,64,128]{2,1,0:T(8,128)}) custom-call(f32[4]{0:T(128)} %levels.1, s32[2,64,128]{2,1,0:T(8,128)} %labels_hbm.1, bf16[64,2,64,128]{3,2,1,0:T(8,128)(2,1)} %z_hbm.1, f32[2,64,128]{2,1,0:T(8,128)} %resid_hbm.1), custom_call_target="tpu_custom_call" | custom-call | tf_op jit(solution)/shard_map/deflated_coarse/pallas_call | solution.py:371
  49.2 1.1 %copy.8 = f32[1,64]{1,0:T(1,128)} copy(f32[1,64]{1,0:T(1,128)} %get-tuple-element.4) | data formatting | bytes 512
  50.3 1.5 %copy.9 = f32[2,64,128]{2,1,0:T(8,128)} copy(f32[2,64,128]{2,1,0:T(8,128)} %get-tuple-element.5) | data formatting | bytes 131072

commit v2 on v1

v2 whole, which is shorter than its diff:
```python
import functools
import math

import jax
import jax.numpy as jnp
from jax import lax
from jax.experimental import pallas as pl
from jax.experimental.pallas import tpu as pltpu
from jax.sharding import PartitionSpec as P

MESH = pl.DeviceIdType.MESH
PRECISE = lax.Precision.HIGHEST
ZCHUNKS = 4
STEP = 4
SLOT = 16
RR, DQ, UU, UQ, QQ, S1, S2, S3 = range(8)


def harmonic(left_value, right_value):
    return 2.0 * left_value * right_value / (left_value + right_value)


def kernel(
    sides,
    levels,
    labels_hbm,
    z_hbm,
    resid_hbm,
    sol_ref,
    defl_ref,
    z,
    lab,
    res,
    lab_send,
    lab_x,
    field,
    field_x,
    edge_send,
    edge,
    edge_modes,
    spread,
    part,
    rows,
    near,
    wide,
    wts,
    load_sem,
    side_send,
    side_recv,
    row_send,
    row_recv,
    sum_send,
    sum_recv,
):
    ny, nz, npln = sides
    nsub = ny * nz * 2
    modes, planes, height, depth = z.shape
    tiles = planes * height // 8
    per_plane = height // 8
    sub = lax.axis_index("sub")
    pln = lax.axis_index("pln")
    core = sub % 2
    zc = (sub // 2) % nz
    yc = sub // (2 * nz)
    first_pln = pln == 0
    last_pln = pln == npln - 1

    per = modes // ZCHUNKS
    res_copy = pltpu.make_async_copy(resid_hbm, res, load_sem.at[0])
    lab_copy = pltpu.make_async_copy(labels_hbm, lab, load_sem.at[1])
    big = [
        pltpu.make_async_copy(
            z_hbm.at[pl.ds(i * per, per)], z.at[pl.ds(i * per, per)], load_sem.at[2 + i]
        )
        for i in range(ZCHUNKS)
    ]
    res_copy.start()
    for copy in big:
        copy.start()
    lab_copy.start()

    halves = npln // 2
    half = pln // 2
    near_count, near_me = 2 * nz, (pln % 2) * nz + zc
    wide_count, wide_me = halves * ny * 2, (half * ny + yc) * 2 + core
    near_peers = []
    for off in range(1, near_count):
        other = (near_me + off) % near_count
        near_peers.append(
            ((yc * nz + other % nz) * 2 + core, pln - pln % 2 + other // nz)
        )
    wide_peers = []
    for off in range(1, wide_count):
        other = (wide_me + off) % wide_count
        apart = other // (2 * ny) - half
        wide_peers.append(
            (
                (((other // 2) % ny) * nz + zc) * 2 + other % 2,
                pln + apart * apart * (npln - 1 - 2 * pln),
            )
        )
    ahead = ((sub + 1) % nsub, pln)
    behind = ((sub + nsub - 1) % nsub, pln)
    right = (sub, (pln + 1) % npln)
    left = (sub, (pln + npln - 1) % npln)
    across = [(sub, (pln + off) % npln) for off in range(1, npln)]
    others = [((sub + 2 * core + nsub - 1) % nsub, pln)] + near_peers + wide_peers
    if halves > 1:
        others.append((sub, (pln + 2) % npln))

    barrier = pltpu.get_barrier_semaphore()
    for peer in others:
        pl.semaphore_signal(barrier, inc=1, device_id=peer, device_id_type=MESH)

    def remote(src, dst, send, recv, target):
        return pltpu.make_async_remote_copy(
            src_ref=src, dst_ref=dst, send_sem=send, recv_sem=recv,
            device_id=target, device_id_type=MESH,
        )

    pending = []

    def plane_copies(which, src, dst):
        copies = [
            remote(src.at[planes - 1], dst.at[0], side_send.at[which, 0],
                   side_recv.at[which, 0], right),
            remote(src.at[0], dst.at[1], side_send.at[which, 1], side_recv.at[which, 1], left),
        ]
        pending.extend(copies)
        return copies

    def edge_copies(which):
        copies = [
            remote(edge_send.at[which], edge.at[which, i], side_send.at[which, 2 + i],
                   side_recv.at[which, 2 + i], target)
            for i, target in enumerate((ahead, behind))
        ]
        pending.extend(copies)
        return copies

    def rows_send(which, row):
        rows[which, pln] = row
        mine = rows.at[which, pln]
        for peer in across:
            remote(mine, mine, row_send.at[which], row_recv.at[which], peer).start()

    def rows_wait(which):
        both = rows.at[which, pl.ds(0, npln - 1)]
        pltpu.make_async_copy(both, both, row_recv.at[which]).wait()
        result = rows[which, 0]
        for i in range(1, npln):
            result = result + rows[which, i]
        return result

    lane = lax.broadcasted_iota(jnp.int32, (1, depth), 1)
    lane8 = lax.broadcasted_iota(jnp.int32, (8, depth), 1)

    def across_lanes(value):
        return jnp.sum(value, axis=1, keepdims=True)

    def whole(value):
        slim = jnp.sum(value.reshape(-1, 8, depth), axis=0)
        return across_lanes(jnp.sum(slim, axis=0, keepdims=True))

    def tile_of(value, j):
        row = (j % per_plane) * 8
        return value[j // per_plane, row:row + 8, :]

    def pack_edges(value):
        packed = jnp.zeros((8, depth), jnp.float32)
        for j in range(tiles):
            rolled = pltpu.roll(tile_of(value, j), 2 * j + 1, 1)
            packed = jnp.where(lane8 // 2 == j, rolled, packed)
        return packed

    def unpack_behind(packed):
        pieces = [pltpu.roll(packed, (depth - 2 * j) % depth, 1) for j in range(tiles)]
        return jnp.concatenate(pieces, axis=0).reshape(planes, height, depth)

    def unpack_ahead(packed):
        pieces = [pltpu.roll(packed, depth - 2 - 2 * j, 1) for j in range(tiles)]
        return jnp.concatenate(pieces, axis=0).reshape(planes, height, depth)

    def project_some(value, start, stop):
        @pl.loop(start // STEP, stop // STEP)
        def _(block):
            for inner in range(STEP):
                k = block * STEP + inner
                product = z[k].astype(jnp.float32) * value
                slim = jnp.sum(product.reshape(-1, 8, depth), axis=0)
                part[pl.ds(k, 1), :] = jnp.sum(slim, axis=0, keepdims=True)

    def project_row():
        ones = jnp.ones((8, depth), jnp.float32)
        gathered = lax.dot_general(
            ones, part[...], (((1,), (1,)), ((), ())), precision=PRECISE,
            preferred_element_type=jnp.float32,
        )
        row = gathered[:1]
        return jnp.concatenate([row, jnp.zeros((1, depth - modes), jnp.float32)], axis=1)

    def spread_row(row):
        here = lax.broadcasted_iota(jnp.int32, (modes, depth), 0)
        there = lax.broadcasted_iota(jnp.int32, (modes, depth), 1)
        picked = jnp.where(here == there, jnp.broadcast_to(row, (modes, depth)), 0.0)
        spread[...] = jnp.broadcast_to(across_lanes(picked), (modes, depth))

    def expand_edges():
        def some(block, acc):
            for inner in range(8):
                k = block * 8 + inner
                acc = acc + edge_modes[k] * jnp.broadcast_to(spread[pl.ds(k, 1), :], (8, depth))
            return acc

        return lax.fori_loop(0, modes // 8, some, jnp.zeros((8, depth), jnp.float32))

    def expand_plane(plane):
        def some(block, acc):
            for inner in range(STEP):
                k = block * STEP + inner
                scale = jnp.broadcast_to(spread[pl.ds(k, 1), :], (height, depth))
                acc = acc + z[k, plane].astype(jnp.float32) * scale
            return acc

        return lax.fori_loop(0, modes // STEP, some, jnp.zeros((height, depth), jnp.float32))

    def expand(which, row):
        spread_row(row)
        edge_send[which + 1] = expand_edges()
        edges = edge_copies(which + 1)
        for copy in edges:
            copy.start()
        sides_x = plane_copies(which + 1, field.at[which], field_x.at[which])
        field[which, 0] = expand_plane(0)
        sides_x[1].start()
        for plane in range(1, planes):
            field[which, plane] = expand_plane(plane)
        sides_x[0].start()
        return edges + sides_x

    y_index = lax.broadcasted_iota(jnp.int32, (planes, height, depth), 1)
    z_index = lax.broadcasted_iota(jnp.int32, (planes, height, depth), 2)

    def along_z(value, before, after):
        low = jnp.where(z_index == 0, unpack_behind(before), pltpu.roll(value, 1, 2))
        high = jnp.where(
            z_index == depth - 1, unpack_ahead(after), pltpu.roll(value, depth - 1, 2)
        )
        return low, high

    def stencil(which):
        value = field[which]
        zero = jnp.zeros_like(value)
        x_low = jnp.where(first_pln, 0.0, field_x[which, 0])
        x_high = jnp.where(last_pln, 0.0, field_x[which, 1])
        x_below = jnp.concatenate([x_low[None], value[:-1]], axis=0)
        x_above = jnp.concatenate([value[1:], x_high[None]], axis=0)
        y_below = jnp.where(y_index == 0, zero, pltpu.roll(value, 1, 1))
        y_above = jnp.where(y_index == height - 1, zero, pltpu.roll(value, height - 1, 1))
        z_below, z_above = along_z(value, edge[which + 1, 0], edge[which + 1, 1])
        return (
            wts[0] * (value - x_below)
            + wts[1] * (value - x_above)
            + wts[2] * (value - y_below)
            + wts[3] * (value - y_above)
            + wts[4] * (value - z_below)
            + wts[5] * (value - z_above)
        )

    res_copy.wait()
    for i in range(ZCHUNKS):
        big[i].wait()
        project_some(res[...], i * per, (i + 1) * per)
    rhs_part = project_row()
    pl.semaphore_wait(barrier, len(others))
    rows_send(0, rhs_part)

    lab_copy.wait()
    narrow = lab[...].astype(jnp.float32)
    lab_send[...] = narrow.astype(jnp.bfloat16)
    edge_send[0] = pack_edges(narrow)
    label_copies = edge_copies(0) + plane_copies(0, lab_send, lab_x)
    for copy in label_copies:
        copy.start()

    @pl.loop(0, modes // 2)
    def _(block):
        for inner in range(2):
            k = block * 2 + inner
            edge_modes[k] = pack_edges(z[k].astype(jnp.float32))

    def density(labels):
        value = jnp.full(labels.shape, levels[0], jnp.float32)
        for i in range(1, levels.shape[0]):
            value = jnp.where(labels == float(i), levels[i], value)
        return value

    for copy in label_copies:
        copy.wait_recv()
    coef = density(lab[...].astype(jnp.float32))
    low = jnp.where(first_pln, coef[0], density(lab_x[0].astype(jnp.float32)))
    high = jnp.where(last_pln, coef[planes - 1], density(lab_x[1].astype(jnp.float32)))
    wts[0] = harmonic(coef, jnp.concatenate([low[None], coef[:-1]], axis=0))
    wts[1] = harmonic(coef, jnp.concatenate([coef[1:], high[None]], axis=0))
    wts[2] = harmonic(coef, jnp.where(y_index == 0, coef, pltpu.roll(coef, 1, 1)))
    wts[3] = harmonic(
        coef, jnp.where(y_index == height - 1, coef, pltpu.roll(coef, height - 1, 1))
    )
    z_low, z_high = along_z(coef, density(edge[0, 0]), density(edge[0, 1]))
    wts[4] = harmonic(coef, z_low)
    wts[5] = harmonic(coef, z_high)

    rhs = rows_wait(0)
    for copy in expand(0, rhs):
        copy.wait_recv()
    image = stencil(0)
    project_some(image, 0, modes)
    rows_send(1, project_row())

    image_row = rows_wait(1)
    copies = expand(1, image_row)
    dq = across_lanes(rhs * image_row)
    qq = across_lanes(image_row * image_row)
    guess = jnp.where(qq > 0.0, dq / jnp.where(qq > 0.0, qq, 1.0), 0.0)
    rest = rhs - guess * image_row
    shared = {
        RR: across_lanes(rhs * rhs),
        DQ: dq,
        UU: across_lanes(rest * rest),
        UQ: across_lanes(rest * image_row),
        QQ: qq,
    }
    spot = lane - SLOT * zc
    packet = jnp.zeros((1, depth), jnp.float32)
    for i, value in shared.items():
        packet = jnp.where(spot == i, jnp.where(first_pln, value, 0.0), packet)
    guesses = jnp.where(
        jnp.logical_and(spot >= 0, spot < SLOT), jnp.where(first_pln, guess, 0.0), 0.0
    )
    for copy in copies:
        copy.wait_recv()
    image_next = stencil(1)
    guess3 = guess[:, :, None]
    rest_field = field[0] - guess3 * field[1]
    rest_image = image - guess3 * image_next
    local = {
        S1: whole(rest_field * rest_image),
        S2: whole(rest_field * image_next + field[1] * rest_image),
        S3: whole(field[1] * image_next),
    }
    for i, value in local.items():
        packet = jnp.where(spot == i, value, packet)

    near[near_me] = jnp.concatenate([packet, guesses], axis=0)
    mine = near.at[near_me]
    for peer in near_peers:
        remote(mine, mine, sum_send.at[0], sum_recv.at[0], peer).start()
    both = near.at[pl.ds(0, near_count - 1)]
    pltpu.make_async_copy(both, both, sum_recv.at[0]).wait()
    wide[wide_me] = jnp.sum(near[...], axis=0)
    mine = wide.at[wide_me]
    for peer in wide_peers:
        remote(mine, mine, sum_send.at[1], sum_recv.at[1], peer).start()
    both = wide.at[pl.ds(0, wide_count - 1)]
    pltpu.make_async_copy(both, both, sum_recv.at[1]).wait()
    count = wide_count // halves
    pairs = []
    for i in range(count):
        pair = wide[i]
        for j in range(1, halves):
            pair = pair + wide[j * count + i]
        pairs.append(pair)
    table = jnp.concatenate(pairs, axis=0)
    shape = table.shape
    upper = lax.broadcasted_iota(jnp.int32, shape, 0) % 2 == 0
    kind = jnp.where(upper, lax.broadcasted_iota(jnp.int32, shape, 1) % SLOT, SLOT)
    step_guess = pltpu.roll(table, shape[0] - 1, 0)

    def total(value):
        return across_lanes(jnp.sum(value, axis=0, keepdims=True))

    norm = total(jnp.where(kind == RR, table, 0.0))
    curve = total(jnp.where(kind == DQ, table, 0.0))
    alpha = norm / curve
    delta = alpha - step_guess
    squared = delta * delta * table
    norm_next = total(
        jnp.where(kind == UU, table, 0.0)
        + jnp.where(kind == UQ, -2.0 * delta * table, 0.0)
        + jnp.where(kind == QQ, squared, 0.0)
    )
    curve_rest = total(
        jnp.where(kind == S1, table, 0.0)
        + jnp.where(kind == S2, -delta * table, 0.0)
        + jnp.where(kind == S3, squared, 0.0)
    )
    mixed = total(
        jnp.where(kind == UQ, table, 0.0) + jnp.where(kind == QQ, -delta * table, 0.0)
    )
    beta = norm_next / norm
    curve_next = curve_rest + 2.0 * beta * mixed + beta * beta * curve
    alpha_next = norm_next / curve_next
    first_part = alpha + alpha_next * (1.0 + beta)
    second_part = alpha_next * alpha
    solution_row = first_part * rhs - second_part * image_row
    sol_ref[...] = solution_row[:, :modes]
    defl_ref[...] = (
        res[...] - first_part[:, :, None] * image + second_part[:, :, None] * image_next
    )

    for copy in pending:
        copy.wait_send()
    for which in range(2):
        both = rows.at[which, pl.ds(0, npln - 1)]
        pltpu.make_async_copy(both, both, row_send.at[which]).wait()
    both = near.at[pl.ds(0, near_count - 1)]
    pltpu.make_async_copy(both, both, sum_send.at[0]).wait()
    both = wide.at[pl.ds(0, wide_count - 1)]
    pltpu.make_async_copy(both, both, sum_send.at[1]).wait()


def body(sides, labels, levels, zvec, resid):
    modes = zvec.shape[0]
    block = resid.shape
    ny, nz, npln = sides
    lanes = block[-1]
    in_hbm = pl.BlockSpec(memory_space=pltpu.HBM)
    vmem = pl.BlockSpec(memory_space=pltpu.VMEM)
    dma = pltpu.SemaphoreType.DMA
    wide = jnp.float32
    return pl.pallas_call(
        functools.partial(kernel, sides),
        out_shape=(
            jax.ShapeDtypeStruct((1, modes), wide),
            jax.ShapeDtypeStruct(block, wide),
        ),
        in_specs=[pl.BlockSpec(memory_space=pltpu.SMEM), in_hbm, in_hbm, in_hbm],
        out_specs=(vmem, vmem),
        scratch_shapes=[
            pltpu.VMEM(zvec.shape, zvec.dtype),
            pltpu.VMEM(block, labels.dtype),
            pltpu.VMEM(block, wide),
            pltpu.VMEM(block, jnp.bfloat16),
            pltpu.VMEM((2,) + block[1:], jnp.bfloat16),
            pltpu.VMEM((2,) + block, wide),
            pltpu.VMEM((2, 2) + block[1:], wide),
            pltpu.VMEM((3, 8, lanes), wide),
            pltpu.VMEM((3, 2, 8, lanes), wide),
            pltpu.VMEM((modes, 8, lanes), wide),
            pltpu.VMEM((modes, lanes), wide),
            pltpu.VMEM((modes, lanes), wide),
            pltpu.VMEM((2, npln, 1, lanes), wide),
            pltpu.VMEM((2 * nz, 2, lanes), wide),
            pltpu.VMEM((npln * ny, 2, lanes), wide),
            pltpu.VMEM((6,) + block, wide),
            dma((2 + ZCHUNKS,)),
            dma((3, 4)),
            dma((3, 4)),
            dma((2,)),
            dma((2,)),
            dma((2,)),
            dma((2,)),
        ],
        compiler_params=pltpu.CompilerParams(
            collective_id=0, has_side_effects=True, vmem_limit_bytes=63 << 20
        ),
        name="deflated_coarse",
    )(levels, labels, zvec, resid)


def solution(mesh):
    chips = mesh.shape["sub"] // 2
    side = math.isqrt(chips)
    sides = (chips // side, side, mesh.shape["pln"])
    in_specs = (P("pln", None, "sub"), P(), P(None, "pln", None, "sub"), P("pln", None, "sub"))
    out_specs = (P("sub", None), P("pln", None, "sub"))
    return jax.shard_map(
        functools.partial(body, sides), mesh=mesh, in_specs=in_specs, out_specs=out_specs,
        check_vma=False,
    )
```

time: 52.6 us -> 47.7 us (0.907); the launches traced: 51.8 us -> 47.5 us
  Pallas kernels: 48.6 us -> 44.2 us
    pallas_call x1, Pallas kernels: 48.6 us -> 44.2 us  [body(): pl.pallas_call(functools.partial(kernel, sides), out_shape=(jax.ShapeDtyp...]
where the time goes in v2:
time: 47.7 us; the launch traced here: 47.5 us
  Pallas kernels  44.2 us (93%)
  local copies, waits for them, and re-layouts  2.59 us (5%)
  between operations  0.64 us (1%)
    pallas_call x1, Pallas kernels, body(): pl.pallas_call(functools.partial(kernel, sides), out_shape=(jax.ShapeDtyp...  44.2 us
    unnamed x2, local copies, waits for them, and re-layouts  2.59 us

profile of v2, /device:TPU:1, one launch (start us, length us, event | category | flops | bytes accessed | tf_op | source)
XLA Modules:
  0.0 47.5 jit_solution(11610130938499497658)
XLA Ops:
  0.6 44.2 %deflated_coarse.1 = (f32[1,64]{1,0:T(1,128)}, f32[2,64,128]{2,1,0:T(8,128)}) custom-call(f32[4]{0:T(128)} %levels.1, s32[2,64,128]{2,1,0:T(8,128)} %labels_hbm.1, bf16[64,2,64,128]{3,2,1,0:T(8,128)(2,1)} %z_hbm.1, f32[2,64,128]{2,1,0:T(8,128)} %resid_hbm.1), custom_call_target="tpu_custom_call" | custom-call | tf_op jit(solution)/shard_map/deflated_coarse/pallas_call | solution.py:431
  44.9 1.1 %copy.8 = f32[1,64]{1,0:T(1,128)} copy(f32[1,64]{1,0:T(1,128)} %get-tuple-element.4) | data formatting | bytes 512
  46.0 1.5 %copy.9 = f32[2,64,128]{2,1,0:T(8,128)} copy(f32[2,64,128]{2,1,0:T(8,128)} %get-tuple-element.5) | data formatting | bytes 131072

commit v3 on v2

--- a/solution.py
+++ b/solution.py
@@ -1,4 +1,5 @@
 import functools
+import itertools
 import math
 
 import jax
@@ -11,7 +12,7 @@
 MESH = pl.DeviceIdType.MESH
 PRECISE = lax.Precision.HIGHEST
 ZCHUNKS = 4
-STEP = 4
+STEP = 16
 SLOT = 16
 RR, DQ, UU, UQ, QQ, S1, S2, S3 = range(8)
 
@@ -22,7 +23,7 @@
 
 def kernel(
     sides,
-    levels,
+    levels_hbm,
     labels_hbm,
     z_hbm,
     resid_hbm,
@@ -34,6 +35,7 @@
     lab_send,
     lab_x,
     field,
+    field_send,
     field_x,
     edge_send,
     edge,
@@ -44,6 +46,7 @@
     near,
     wide,
     wts,
+    levels,
     load_sem,
     side_send,
     side_recv,
@@ -59,9 +62,9 @@
     per_plane = height // 8
     sub = lax.axis_index("sub")
     pln = lax.axis_index("pln")
-    core = sub % 2
-    zc = (sub // 2) % nz
-    yc = sub // (2 * nz)
+    core = lax.rem(sub, 2)
+    zc = lax.rem(lax.div(sub, 2), nz)
+    yc = lax.div(sub, 2 * nz)
     first_pln = pln == 0
     last_pln = pln == npln - 1
 
@@ -78,35 +81,40 @@
     for copy in big:
         copy.start()
     lab_copy.start()
+    level_copy = pltpu.make_async_copy(levels_hbm, levels, load_sem.at[2 + ZCHUNKS])
+    level_copy.start()
 
     halves = npln // 2
-    half = pln // 2
-    near_count, near_me = 2 * nz, (pln % 2) * nz + zc
+    odd, half = lax.rem(pln, 2), lax.div(pln, 2)
+    near_count, near_me = 2 * nz, odd * nz + zc
     wide_count, wide_me = halves * ny * 2, (half * ny + yc) * 2 + core
-    near_peers = []
-    for off in range(1, near_count):
-        other = (near_me + off) % near_count
-        near_peers.append(
-            ((yc * nz + other % nz) * 2 + core, pln - pln % 2 + other // nz)
+
+    def offsets(*sizes):
+        def hops(offset):
+            return sum(min(step, size - step) for step, size in zip(offset, sizes))
+
+        every = list(itertools.product(*(range(size) for size in sizes)))
+        return sorted(every[1:], key=hops, reverse=True)
+
+    near_peers = [
+        (sub - 2 * zc + 2 * lax.rem(zc + step, nz), pln + flip * (1 - 2 * odd))
+        for flip, step in offsets(2, nz)
+    ]
+    wide_peers = [
+        (
+            (lax.rem(yc + step, ny) * nz + zc) * 2 + (1 - core if other else core),
+            npln - 1 - pln if flip else pln,
         )
-    wide_peers = []
-    for off in range(1, wide_count):
-        other = (wide_me + off) % wide_count
-        apart = other // (2 * ny) - half
-        wide_peers.append(
-            (
-                (((other // 2) % ny) * nz + zc) * 2 + other % 2,
-                pln + apart * apart * (npln - 1 - 2 * pln),
-            )
-        )
-    ahead = ((sub + 1) % nsub, pln)
-    behind = ((sub + nsub - 1) % nsub, pln)
-    right = (sub, (pln + 1) % npln)
-    left = (sub, (pln + npln - 1) % npln)
-    across = [(sub, (pln + off) % npln) for off in range(1, npln)]
-    others = [((sub + 2 * core + nsub - 1) % nsub, pln)] + near_peers + wide_peers
+        for flip, step, other in offsets(halves, ny, 2)
+    ]
+    ahead = (lax.rem(sub + 1, nsub), pln)
+    behind = (lax.rem(sub + nsub - 1, nsub), pln)
+    right = (sub, lax.rem(pln + 1, npln))
+    left = (sub, lax.rem(pln + npln - 1, npln))
+    across = [(sub, lax.rem(pln + off, npln)) for off in (2, 1, 3) if off < npln]
+    others = [(lax.rem(sub + 2 * core + nsub - 1, nsub), pln)] + near_peers + wide_peers
     if halves > 1:
-        others.append((sub, (pln + 2) % npln))
+        others.append((sub, lax.rem(pln + 2, npln)))
 
     barrier = pltpu.get_barrier_semaphore()
     for peer in others:
@@ -230,11 +238,13 @@
         edges = edge_copies(which + 1)
         for copy in edges:
             copy.start()
-        sides_x = plane_copies(which + 1, field.at[which], field_x.at[which])
-        field[which, 0] = expand_plane(0)
-        sides_x[1].start()
-        for plane in range(1, planes):
-            field[which, plane] = expand_plane(plane)
+        sides_x = plane_copies(which + 1, field_send.at[which], field_x.at[which])
+        for plane in range(planes):
+            value = expand_plane(plane)
+            field[which, plane] = value
+            field_send[which, plane] = value.astype(jnp.bfloat16)
+            if plane == 0:
+                sides_x[1].start()
         sides_x[0].start()
         return edges + sides_x
 
@@ -251,8 +261,8 @@
     def stencil(which):
         value = field[which]
         zero = jnp.zeros_like(value)
-        x_low = jnp.where(first_pln, 0.0, field_x[which, 0])
-        x_high = jnp.where(last_pln, 0.0, field_x[which, 1])
+        x_low = jnp.where(first_pln, 0.0, field_x[which, 0].astype(jnp.float32))
+        x_high = jnp.where(last_pln, 0.0, field_x[which, 1].astype(jnp.float32))
         x_below = jnp.concatenate([x_low[None], value[:-1]], axis=0)
         x_above = jnp.concatenate([value[1:], x_high[None]], axis=0)
         y_below = jnp.where(y_index == 0, zero, pltpu.roll(value, 1, 1))
@@ -276,6 +286,7 @@
     rows_send(0, rhs_part)
 
     lab_copy.wait()
+    level_copy.wait()
     narrow = lab[...].astype(jnp.float32)
     lab_send[...] = narrow.astype(jnp.bfloat16)
     edge_send[0] = pack_edges(narrow)
@@ -283,10 +294,10 @@
     for copy in label_copies:
         copy.start()
 
-    @pl.loop(0, modes // 2)
+    @pl.loop(0, modes // 8)
     def _(block):
-        for inner in range(2):
-            k = block * 2 + inner
+        for inner in range(8):
+            k = block * 8 + inner
             edge_modes[k] = pack_edges(z[k].astype(jnp.float32))
 
     def density(labels):
@@ -295,6 +306,8 @@
             value = jnp.where(labels == float(i), levels[i], value)
         return value
 
+    rhs = rows_wait(0)
+    copies = expand(0, rhs)
     for copy in label_copies:
         copy.wait_recv()
     coef = density(lab[...].astype(jnp.float32))
@@ -310,8 +323,7 @@
     wts[4] = harmonic(coef, z_low)
     wts[5] = harmonic(coef, z_high)
 
-    rhs = rows_wait(0)
-    for copy in expand(0, rhs):
+    for copy in copies:
         copy.wait_recv()
     image = stencil(0)
     project_some(image, 0, modes)
@@ -419,6 +431,17 @@
     pltpu.make_async_copy(both, both, sum_send.at[1]).wait()
 
 
+def finish(row, out, sol_hbm, defl_hbm, sems):
+    copies = [
+        pltpu.make_async_copy(out, defl_hbm, sems.at[0]),
+        pltpu.make_async_copy(row, sol_hbm, sems.at[1]),
+    ]
+    for copy in copies:
+        copy.start()
+    for copy in copies:
+        copy.wait()
+
+
 def body(sides, labels, levels, zvec, resid):
     modes = zvec.shape[0]
     block = resid.shape
@@ -428,13 +451,13 @@
     vmem = pl.BlockSpec(memory_space=pltpu.VMEM)
     dma = pltpu.SemaphoreType.DMA
     wide = jnp.float32
-    return pl.pallas_call(
+    row, out = pl.pallas_call(
         functools.partial(kernel, sides),
         out_shape=(
             jax.ShapeDtypeStruct((1, modes), wide),
             jax.ShapeDtypeStruct(block, wide),
         ),
-        in_specs=[pl.BlockSpec(memory_space=pltpu.SMEM), in_hbm, in_hbm, in_hbm],
+        in_specs=[in_hbm] * 4,
         out_specs=(vmem, vmem),
         scratch_shapes=[
             pltpu.VMEM(zvec.shape, zvec.dtype),
@@ -443,7 +466,8 @@
             pltpu.VMEM(block, jnp.bfloat16),
             pltpu.VMEM((2,) + block[1:], jnp.bfloat16),
             pltpu.VMEM((2,) + block, wide),
-            pltpu.VMEM((2, 2) + block[1:], wide),
+            pltpu.VMEM((2,) + block, jnp.bfloat16),
+            pltpu.VMEM((2, 2) + block[1:], jnp.bfloat16),
             pltpu.VMEM((3, 8, lanes), wide),
             pltpu.VMEM((3, 2, 8, lanes), wide),
             pltpu.VMEM((modes, 8, lanes), wide),
@@ -453,7 +477,8 @@
             pltpu.VMEM((2 * nz, 2, lanes), wide),
             pltpu.VMEM((npln * ny, 2, lanes), wide),
             pltpu.VMEM((6,) + block, wide),
-            dma((2 + ZCHUNKS,)),
+            pltpu.SMEM(levels.shape, wide),
+            dma((3 + ZCHUNKS,)),
             dma((3, 4)),
             dma((3, 4)),
             dma((2,)),
@@ -462,10 +487,24 @@
             dma((2,)),
         ],
         compiler_params=pltpu.CompilerParams(
-            collective_id=0, has_side_effects=True, vmem_limit_bytes=63 << 20
+            collective_id=0, has_side_effects=True, vmem_limit_bytes=24 << 20
         ),
         name="deflated_coarse",
-    )(levels, labels, zvec, resid)
+    )(
+        *(pltpu.with_memory_space_constraint(a, pltpu.HBM) for a in (levels, labels, zvec, resid))
+    )
+    return pl.pallas_call(
+        finish,
+        out_shape=(
+            jax.ShapeDtypeStruct((1, modes), wide),
+            jax.ShapeDtypeStruct(block, wide),
+        ),
+        in_specs=[vmem, vmem],
+        out_specs=(in_hbm, in_hbm),
+        scratch_shapes=[dma((2,))],
+        compiler_params=pltpu.CompilerParams(vmem_limit_bytes=2 << 20),
+        name="finish",
+    )(row, out)
 
 
 def solution(mesh):

time: 47.7 us -> 42.8 us (0.90)
  local copies, waits for them, and re-layouts: 2.59 us -> 0 us
  Pallas kernels: 44.2 us -> 42 us
    pallas_call x1, Pallas kernels: 44.2 us -> 41.4 us  [body(): pl.pallas_call(functools.partial(kernel, sides), out_shape=(jax.ShapeDtyp...]
    unnamed x2 -> x0, local copies, waits for them, and re-layouts: 2.59 us -> none
    pallas_call x0 -> x1, Pallas kernels: none -> 0.65 us  [body(): pl.pallas_call(finish, out_shape=(jax.ShapeDtypeStruct((1, modes), wide),...]
where the time goes in v3:
time: 42.8 us; the launch traced here: 42.7 us
  Pallas kernels  42 us (98%)
  between operations  0.64 us (1%)
    pallas_call x1, Pallas kernels, body(): pl.pallas_call(functools.partial(kernel, sides), out_shape=(jax.ShapeDtyp...  41.4 us

profile of v3, /device:TPU:1, one launch (start us, length us, event | category | flops | bytes accessed | tf_op | source)
XLA Modules:
  0.0 42.7 jit_solution(5961281570962837528)
XLA Ops:
  0.6 41.4 %deflated_coarse.1 = (f32[1,64]{1,0:T(1,128)S(1)}, f32[2,64,128]{2,1,0:T(8,128)S(1)}) custom-call(f32[4]{0:T(128)} %levels_hbm.1, s32[2,64,128]{2,1,0:T(8,128)} %labels_hbm.1, bf16[64,2,64,128]{3,2,1,0:T(8,128)(2,1)} %z_hbm.1, f32[2,64,128]{2,1,0:T(8,128)} %resid_hbm.1), custom_call_target="tpu_custom_call" | custom-call | tf_op jit(solution)/shard_map/deflated_coarse/pallas_call | solution.py:454
  42.0 0.7 %finish.1 = (f32[1,64]{1,0:T(1,128)}, f32[2,64,128]{2,1,0:T(8,128)}) custom-call(f32[1,64]{1,0:T(1,128)S(1)} %get-tuple-element.4.row, f32[2,64,128]{2,1,0:T(8,128)S(1)} %get-tuple-element.5.out), custom_call_target="tpu_custom_call" | custom-call | tf_op jit(solution)/shard_map/finish/pallas_call | solution.py:496

commit v4 on v3

--- a/solution.py
+++ b/solution.py
@@ -54,6 +54,7 @@
     row_recv,
     sum_send,
     sum_recv,
+    token,
 ):
     ny, nz, npln = sides
     nsub = ny * nz * 2
@@ -112,9 +113,33 @@
     right = (sub, lax.rem(pln + 1, npln))
     left = (sub, lax.rem(pln + npln - 1, npln))
     across = [(sub, lax.rem(pln + off, npln)) for off in (2, 1, 3) if off < npln]
-    others = [(lax.rem(sub + 2 * core + nsub - 1, nsub), pln)] + near_peers + wide_peers
-    if halves > 1:
-        others.append((sub, lax.rem(pln + 2, npln)))
+
+    def beside(axis, steps):
+        if axis == 0:
+            return [
+                (sub + 2 * (lax.rem(zc + step, nz) - zc), pln) for step in (steps, nz - steps)
+            ]
+        return [
+            (sub + 2 * nz * (lax.rem(yc + step, ny) - yc), pln) for step in (steps, ny - steps)
+        ]
+
+    others = [ahead, behind] + across + beside(0, 1) + beside(1, 1)
+    reaches = [[1 << i for i in range((size // 2).bit_length() - 1)] for size in (nz, ny)]
+
+    def tokens_send(turn):
+        for axis, reach in enumerate(reaches):
+            if turn < len(reach):
+                for peer in beside(axis, reach[turn]):
+                    pl.semaphore_signal(
+                        token.at[axis, turn], inc=1, device_id=peer, device_id_type=MESH
+                    )
+
+    def tokens_wait(turn):
+        for axis, reach in enumerate(reaches):
+            if turn < len(reach):
+                pl.semaphore_wait(token.at[axis, turn], 2)
+
+    turns = max(len(reach) for reach in reaches)
 
     barrier = pltpu.get_barrier_semaphore()
     for peer in others:
@@ -284,6 +309,8 @@
     rhs_part = project_row()
     pl.semaphore_wait(barrier, len(others))
     rows_send(0, rhs_part)
+    if turns > 0:
+        tokens_send(0)
 
     lab_copy.wait()
     level_copy.wait()
@@ -308,6 +335,9 @@
 
     rhs = rows_wait(0)
     copies = expand(0, rhs)
+    for turn in range(1, turns):
+        tokens_wait(turn - 1)
+        tokens_send(turn)
     for copy in label_copies:
         copy.wait_recv()
     coef = density(lab[...].astype(jnp.float32))
@@ -327,6 +357,8 @@
         copy.wait_recv()
     image = stencil(0)
     project_some(image, 0, modes)
+    if turns > 0:
+        tokens_wait(turns - 1)
     rows_send(1, project_row())
 
     image_row = rows_wait(1)
@@ -485,6 +517,7 @@
             dma((2,)),
             dma((2,)),
             dma((2,)),
+            pltpu.SemaphoreType.REGULAR((2, 4)),
         ],
         compiler_params=pltpu.CompilerParams(
             collective_id=0, has_side_effects=True, vmem_limit_bytes=24 << 20

time: 42.8 us -> 41 us (0.958)
  Pallas kernels: 42 us -> 40.2 us
    pallas_call x1, Pallas kernels: 41.4 us -> 39.5 us  [body(): pl.pallas_call(functools.partial(kernel, sides), out_shape=(jax.ShapeDtyp...]
where the time goes in v4:
time: 41 us; the launch traced here: 40.8 us
  Pallas kernels  40.2 us (98%)
  between operations  0.64 us (2%)
    pallas_call x1, Pallas kernels, body(): pl.pallas_call(functools.partial(kernel, sides), out_shape=(jax.ShapeDtyp...  39.5 us

profile of v4, /device:TPU:1, one launch (start us, length us, event | category | flops | bytes accessed | tf_op | source)
XLA Modules:
  0.0 40.8 jit_solution(15045410974302117789)
XLA Ops:
  0.6 39.5 %deflated_coarse.1 = (f32[1,64]{1,0:T(1,128)S(1)}, f32[2,64,128]{2,1,0:T(8,128)S(1)}) custom-call(f32[4]{0:T(128)} %levels_hbm.1, s32[2,64,128]{2,1,0:T(8,128)} %labels_hbm.1, bf16[64,2,64,128]{3,2,1,0:T(8,128)(2,1)} %z_hbm.1, f32[2,64,128]{2,1,0:T(8,128)} %resid_hbm.1), custom_call_target="tpu_custom_call" | custom-call | tf_op jit(solution)/shard_map/deflated_coarse/pallas_call | solution.py:486
  40.2 0.7 %finish.1 = (f32[1,64]{1,0:T(1,128)}, f32[2,64,128]{2,1,0:T(8,128)}) custom-call(f32[1,64]{1,0:T(1,128)S(1)} %get-tuple-element.4.row, f32[2,64,128]{2,1,0:T(8,128)S(1)} %get-tuple-element.5.out), custom_call_target="tpu_custom_call" | custom-call | tf_op jit(solution)/shard_map/finish/pallas_call | solution.py:529

commit v5 on v4

--- a/solution.py
+++ b/solution.py
@@ -11,9 +11,9 @@
 
 MESH = pl.DeviceIdType.MESH
 PRECISE = lax.Precision.HIGHEST
-ZCHUNKS = 4
-STEP = 16
-SLOT = 16
+ZCHUNKS = 8
+STEP = 8
+SLOT = 8
 RR, DQ, UU, UQ, QQ, S1, S2, S3 = range(8)
 
 
@@ -30,6 +30,7 @@
     sol_ref,
     defl_ref,
     z,
+    zf,
     lab,
     res,
     lab_send,
@@ -87,8 +88,9 @@
 
     halves = npln // 2
     odd, half = lax.rem(pln, 2), lax.div(pln, 2)
-    near_count, near_me = 2 * nz, odd * nz + zc
-    wide_count, wide_me = halves * ny * 2, (half * ny + yc) * 2 + core
+    place = yc * 2 + core
+    near_count, near_me = 4 * ny, odd * 2 * ny + place
+    wide_count, wide_me = halves * nz, half * nz + zc
 
     def offsets(*sizes):
         def hops(offset):
@@ -98,15 +100,18 @@
         return sorted(every[1:], key=hops, reverse=True)
 
     near_peers = [
-        (sub - 2 * zc + 2 * lax.rem(zc + step, nz), pln + flip * (1 - 2 * odd))
-        for flip, step in offsets(2, nz)
+        (
+            (lax.rem(yc + step, ny) * nz + zc) * 2 + (1 - core if other else core),
+            pln + flip * (1 - 2 * odd),
+        )
+        for flip, step, other in offsets(2, ny, 2)
     ]
     wide_peers = [
         (
-            (lax.rem(yc + step, ny) * nz + zc) * 2 + (1 - core if other else core),
+            sub - 2 * zc + 2 * lax.rem(zc + step, nz),
             npln - 1 - pln if flip else pln,
         )
-        for flip, step, other in offsets(halves, ny, 2)
+        for flip, step in offsets(halves, nz)
     ]
     ahead = (lax.rem(sub + 1, nsub), pln)
     behind = (lax.rem(sub + nsub - 1, nsub), pln)
@@ -214,12 +219,12 @@
         pieces = [pltpu.roll(packed, depth - 2 - 2 * j, 1) for j in range(tiles)]
         return jnp.concatenate(pieces, axis=0).reshape(planes, height, depth)
 
-    def project_some(value, start, stop):
+    def project_some(source, value, start, stop):
         @pl.loop(start // STEP, stop // STEP)
         def _(block):
             for inner in range(STEP):
                 k = block * STEP + inner
-                product = z[k].astype(jnp.float32) * value
+                product = source[k].astype(jnp.float32) * value
                 slim = jnp.sum(product.reshape(-1, 8, depth), axis=0)
                 part[pl.ds(k, 1), :] = jnp.sum(slim, axis=0, keepdims=True)
 
@@ -252,17 +257,14 @@
             for inner in range(STEP):
                 k = block * STEP + inner
                 scale = jnp.broadcast_to(spread[pl.ds(k, 1), :], (height, depth))
-                acc = acc + z[k, plane].astype(jnp.float32) * scale
+                acc = acc + zf[k, plane] * scale
             return acc
 
         return lax.fori_loop(0, modes // STEP, some, jnp.zeros((height, depth), jnp.float32))
 
     def expand(which, row):
         spread_row(row)
-        edge_send[which + 1] = expand_edges()
         edges = edge_copies(which + 1)
-        for copy in edges:
-            copy.start()
         sides_x = plane_copies(which + 1, field_send.at[which], field_x.at[which])
         for plane in range(planes):
             value = expand_plane(plane)
@@ -271,6 +273,9 @@
             if plane == 0:
                 sides_x[1].start()
         sides_x[0].start()
+        edge_send[which + 1] = expand_edges()
+        for copy in edges:
+            copy.start()
         return edges + sides_x
 
     y_index = lax.broadcasted_iota(jnp.int32, (planes, height, depth), 1)
@@ -305,7 +310,7 @@
     res_copy.wait()
     for i in range(ZCHUNKS):
         big[i].wait()
-        project_some(res[...], i * per, (i + 1) * per)
+        project_some(z, res[...], i * per, (i + 1) * per)
     rhs_part = project_row()
     pl.semaphore_wait(barrier, len(others))
     rows_send(0, rhs_part)
@@ -325,7 +330,9 @@
     def _(block):
         for inner in range(8):
             k = block * 8 + inner
-            edge_modes[k] = pack_edges(z[k].astype(jnp.float32))
+            mode = z[k].astype(jnp.float32)
+            zf[k] = mode
+            edge_modes[k] = pack_edges(mode)
 
     def density(labels):
         value = jnp.full(labels.shape, levels[0], jnp.float32)
@@ -356,7 +363,7 @@
     for copy in copies:
         copy.wait_recv()
     image = stencil(0)
-    project_some(image, 0, modes)
+    project_some(zf, image, 0, modes)
     if turns > 0:
         tokens_wait(turns - 1)
     rows_send(1, project_row())
@@ -374,7 +381,7 @@
         UQ: across_lanes(rest * image_row),
         QQ: qq,
     }
-    spot = lane - SLOT * zc
+    spot = lane - SLOT * place
     packet = jnp.zeros((1, depth), jnp.float32)
     for i, value in shared.items():
         packet = jnp.where(spot == i, jnp.where(first_pln, value, 0.0), packet)
@@ -493,6 +500,7 @@
         out_specs=(vmem, vmem),
         scratch_shapes=[
             pltpu.VMEM(zvec.shape, zvec.dtype),
+            pltpu.VMEM(zvec.shape, wide),
             pltpu.VMEM(block, labels.dtype),
             pltpu.VMEM(block, wide),
             pltpu.VMEM(block, jnp.bfloat16),
@@ -506,8 +514,8 @@
             pltpu.VMEM((modes, lanes), wide),
             pltpu.VMEM((modes, lanes), wide),
             pltpu.VMEM((2, npln, 1, lanes), wide),
-            pltpu.VMEM((2 * nz, 2, lanes), wide),
-            pltpu.VMEM((npln * ny, 2, lanes), wide),
+            pltpu.VMEM((4 * ny, 2, lanes), wide),
+            pltpu.VMEM((npln // 2 * nz, 2, lanes), wide),
             pltpu.VMEM((6,) + block, wide),
             pltpu.SMEM(levels.shape, wide),
             dma((3 + ZCHUNKS,)),

time: 41 us -> 40.2 us (0.980)
  Pallas kernels: 40.2 us -> 39.4 us
    pallas_call x1, Pallas kernels: 39.5 us -> 38.8 us  [body(): pl.pallas_call(functools.partial(kernel, sides), out_shape=(jax.ShapeDtyp...]
where the time goes in v5:
time: 40.2 us; the launch traced here: 40.1 us
  Pallas kernels  39.4 us (98%)
  between operations  0.64 us (2%)
    pallas_call x1, Pallas kernels, body(): pl.pallas_call(functools.partial(kernel, sides), out_shape=(jax.ShapeDtyp...  38.8 us

profile of v5, /device:TPU:1, one launch (start us, length us, event | category | flops | bytes accessed | tf_op | source)
XLA Modules:
  0.0 40.1 jit_solution(7648410474753546920)
XLA Ops:
  0.6 38.8 %deflated_coarse.1 = (f32[1,64]{1,0:T(1,128)S(1)}, f32[2,64,128]{2,1,0:T(8,128)S(1)}) custom-call(f32[4]{0:T(128)} %levels_hbm.1, s32[2,64,128]{2,1,0:T(8,128)} %labels_hbm.1, bf16[64,2,64,128]{3,2,1,0:T(8,128)(2,1)} %z_hbm.1, f32[2,64,128]{2,1,0:T(8,128)} %resid_hbm.1), custom_call_target="tpu_custom_call" | custom-call | tf_op jit(solution)/shard_map/deflated_coarse/pallas_call | solution.py:493
  39.4 0.7 %finish.1 = (f32[1,64]{1,0:T(1,128)}, f32[2,64,128]{2,1,0:T(8,128)}) custom-call(f32[1,64]{1,0:T(1,128)S(1)} %get-tuple-element.4.row, f32[2,64,128]{2,1,0:T(8,128)S(1)} %get-tuple-element.5.out), custom_call_target="tpu_custom_call" | custom-call | tf_op jit(solution)/shard_map/finish/pallas_call | solution.py:537

commit v6 on v5

--- a/solution.py
+++ b/solution.py
@@ -10,9 +10,8 @@
 from jax.sharding import PartitionSpec as P
 
 MESH = pl.DeviceIdType.MESH
-PRECISE = lax.Precision.HIGHEST
-ZCHUNKS = 8
-STEP = 8
+ZCHUNKS = 4
+STEP = 16
 SLOT = 8
 RR, DQ, UU, UQ, QQ, S1, S2, S3 = range(8)
 
@@ -226,12 +225,20 @@
                 k = block * STEP + inner
                 product = source[k].astype(jnp.float32) * value
                 slim = jnp.sum(product.reshape(-1, 8, depth), axis=0)
-                part[pl.ds(k, 1), :] = jnp.sum(slim, axis=0, keepdims=True)
+                part[pl.ds(pl.multiple_of(k * 8, 8), 8), :] = slim
 
     def project_row():
-        ones = jnp.ones((8, depth), jnp.float32)
+        value = part[pl.ds(0, modes, stride=8), :]
+        for i in range(1, 8):
+            value = value + part[pl.ds(i, modes, stride=8), :]
+        pieces = []
+        for _ in range(3):
+            pieces.append(value.astype(jnp.bfloat16))
+            value = value - pieces[-1].astype(jnp.float32)
         gathered = lax.dot_general(
-            ones, part[...], (((1,), (1,)), ((), ())), precision=PRECISE,
+            jnp.ones((8, 3 * depth), jnp.bfloat16),
+            jnp.concatenate(pieces, axis=1),
+            (((1,), (1,)), ((), ())),
             preferred_element_type=jnp.float32,
         )
         row = gathered[:1]
@@ -412,6 +419,14 @@
     mine = wide.at[wide_me]
     for peer in wide_peers:
         remote(mine, mine, sum_send.at[1], sum_recv.at[1], peer).start()
+    for copy in pending:
+        copy.wait_send()
+    for which in range(2):
+        both = rows.at[which, pl.ds(0, npln - 1)]
+        pltpu.make_async_copy(both, both, row_send.at[which]).wait()
+    both = near.at[pl.ds(0, near_count - 1)]
+    pltpu.make_async_copy(both, both, sum_send.at[0]).wait()
+
     both = wide.at[pl.ds(0, wide_count - 1)]
     pltpu.make_async_copy(both, both, sum_recv.at[1]).wait()
     count = wide_count // halves
@@ -459,13 +474,6 @@
         res[...] - first_part[:, :, None] * image + second_part[:, :, None] * image_next
     )
 
-    for copy in pending:
-        copy.wait_send()
-    for which in range(2):
-        both = rows.at[which, pl.ds(0, npln - 1)]
-        pltpu.make_async_copy(both, both, row_send.at[which]).wait()
-    both = near.at[pl.ds(0, near_count - 1)]
-    pltpu.make_async_copy(both, both, sum_send.at[0]).wait()
     both = wide.at[pl.ds(0, wide_count - 1)]
     pltpu.make_async_copy(both, both, sum_send.at[1]).wait()
 
@@ -512,7 +520,7 @@
             pltpu.VMEM((3, 2, 8, lanes), wide),
             pltpu.VMEM((modes, 8, lanes), wide),
             pltpu.VMEM((modes, lanes), wide),
-            pltpu.VMEM((modes, lanes), wide),
+            pltpu.VMEM((8 * modes, lanes), wide),
             pltpu.VMEM((2, npln, 1, lanes), wide),
             pltpu.VMEM((4 * ny, 2, lanes), wide),
             pltpu.VMEM((npln // 2 * nz, 2, lanes), wide),

time: 40.2 us -> 40 us (level)
  no operation moved by 1% of the time
where the time goes in v6:
time: 40 us; the launch traced here: 39.8 us
  Pallas kernels  39.2 us (98%)
  between operations  0.64 us (2%)
    pallas_call x1, Pallas kernels, body(): pl.pallas_call(functools.partial(kernel, sides), out_shape=(jax.ShapeDtyp...  38.5 us

profile of v6, /device:TPU:1, one launch (start us, length us, event | category | flops | bytes accessed | tf_op | source)
XLA Modules:
  0.0 39.8 jit_solution(10466677355595731653)
XLA Ops:
  0.6 38.5 %deflated_coarse.1 = (f32[1,64]{1,0:T(1,128)S(1)}, f32[2,64,128]{2,1,0:T(8,128)S(1)}) custom-call(f32[4]{0:T(128)} %levels_hbm.1, s32[2,64,128]{2,1,0:T(8,128)} %labels_hbm.1, bf16[64,2,64,128]{3,2,1,0:T(8,128)(2,1)} %z_hbm.1, f32[2,64,128]{2,1,0:T(8,128)} %resid_hbm.1), custom_call_target="tpu_custom_call" | custom-call | tf_op jit(solution)/shard_map/deflated_coarse/pallas_call | solution.py:501
  39.2 0.7 %finish.1 = (f32[1,64]{1,0:T(1,128)}, f32[2,64,128]{2,1,0:T(8,128)}) custom-call(f32[1,64]{1,0:T(1,128)S(1)} %get-tuple-element.4.row, f32[2,64,128]{2,1,0:T(8,128)S(1)} %get-tuple-element.5.out), custom_call_target="tpu_custom_call" | custom-call | tf_op jit(solution)/shard_map/finish/pallas_call | solution.py:545

commit v7 on v6

--- a/solution.py
+++ b/solution.py
@@ -225,12 +225,10 @@
                 k = block * STEP + inner
                 product = source[k].astype(jnp.float32) * value
                 slim = jnp.sum(product.reshape(-1, 8, depth), axis=0)
-                part[pl.ds(pl.multiple_of(k * 8, 8), 8), :] = slim
+                part[pl.ds(k, 1), :] = jnp.sum(slim, axis=0, keepdims=True)
 
     def project_row():
-        value = part[pl.ds(0, modes, stride=8), :]
-        for i in range(1, 8):
-            value = value + part[pl.ds(i, modes, stride=8), :]
+        value = part[...]
         pieces = []
         for _ in range(3):
             pieces.append(value.astype(jnp.bfloat16))
@@ -295,16 +293,16 @@
         )
         return low, high
 
-    def stencil(which):
+    def stencil_inside(which):
         value = field[which]
         zero = jnp.zeros_like(value)
-        x_low = jnp.where(first_pln, 0.0, field_x[which, 0].astype(jnp.float32))
-        x_high = jnp.where(last_pln, 0.0, field_x[which, 1].astype(jnp.float32))
-        x_below = jnp.concatenate([x_low[None], value[:-1]], axis=0)
-        x_above = jnp.concatenate([value[1:], x_high[None]], axis=0)
+        edge_plane = jnp.zeros_like(value[:1])
+        x_below = jnp.concatenate([edge_plane, value[:-1]], axis=0)
+        x_above = jnp.concatenate([value[1:], edge_plane], axis=0)
         y_below = jnp.where(y_index == 0, zero, pltpu.roll(value, 1, 1))
         y_above = jnp.where(y_index == height - 1, zero, pltpu.roll(value, height - 1, 1))
-        z_below, z_above = along_z(value, edge[which + 1, 0], edge[which + 1, 1])
+        z_below = jnp.where(z_index == 0, zero, pltpu.roll(value, 1, 2))
+        z_above = jnp.where(z_index == depth - 1, zero, pltpu.roll(value, depth - 1, 2))
         return (
             wts[0] * (value - x_below)
             + wts[1] * (value - x_above)
@@ -312,6 +310,25 @@
             + wts[3] * (value - y_above)
             + wts[4] * (value - z_below)
             + wts[5] * (value - z_above)
+        )
+
+    def stencil_sides(which, inside):
+        x_low = jnp.where(first_pln, 0.0, field_x[which, 0].astype(jnp.float32))
+        x_high = jnp.where(last_pln, 0.0, field_x[which, 1].astype(jnp.float32))
+        z_below = unpack_behind(edge[which + 1, 0])
+        z_above = unpack_ahead(edge[which + 1, 1])
+        result = (
+            inside
+            - jnp.where(z_index == 0, wts[4] * z_below, 0.0)
+            - jnp.where(z_index == depth - 1, wts[5] * z_above, 0.0)
+        )
+        top = planes - 1
+        if top == 0:
+            return result - (wts[0, 0] * x_low + wts[1, 0] * x_high)[None]
+        first = result[0] - wts[0, 0] * x_low
+        last = result[top] - wts[1, top] * x_high
+        return jnp.concatenate([first[None], result[1:top], last[None]], axis=0) if top > 1 else (
+            jnp.concatenate([first[None], last[None]], axis=0)
         )
 
     res_copy.wait()
@@ -367,9 +384,10 @@
     wts[4] = harmonic(coef, z_low)
     wts[5] = harmonic(coef, z_high)
 
+    inside = stencil_inside(0)
     for copy in copies:
         copy.wait_recv()
-    image = stencil(0)
+    image = stencil_sides(0, inside)
     project_some(zf, image, 0, modes)
     if turns > 0:
         tokens_wait(turns - 1)
@@ -395,9 +413,10 @@
     guesses = jnp.where(
         jnp.logical_and(spot >= 0, spot < SLOT), jnp.where(first_pln, guess, 0.0), 0.0
     )
+    inside = stencil_inside(1)
     for copy in copies:
         copy.wait_recv()
-    image_next = stencil(1)
+    image_next = stencil_sides(1, inside)
     guess3 = guess[:, :, None]
     rest_field = field[0] - guess3 * field[1]
     rest_image = image - guess3 * image_next
@@ -520,7 +539,7 @@
             pltpu.VMEM((3, 2, 8, lanes), wide),
             pltpu.VMEM((modes, 8, lanes), wide),
             pltpu.VMEM((modes, lanes), wide),
-            pltpu.VMEM((8 * modes, lanes), wide),
+            pltpu.VMEM((modes, lanes), wide),
             pltpu.VMEM((2, npln, 1, lanes), wide),
             pltpu.VMEM((4 * ny, 2, lanes), wide),
             pltpu.VMEM((npln // 2 * nz, 2, lanes), wide),

time: 40 us -> 39.9 us (level)
  no operation moved by 1% of the time
where the time goes in v7:
time: 39.9 us; the launch traced here: 39.8 us
  Pallas kernels  39.1 us (98%)
  between operations  0.64 us (2%)
    pallas_call x1, Pallas kernels, body(): pl.pallas_call(functools.partial(kernel, sides), out_shape=(jax.ShapeDtyp...  38.5 us

profile of v7, /device:TPU:1, one launch (start us, length us, event | category | flops | bytes accessed | tf_op | source)
XLA Modules:
  0.0 39.8 jit_solution(9316143244673185132)
XLA Ops:
  0.6 38.5 %deflated_coarse.1 = (f32[1,64]{1,0:T(1,128)S(1)}, f32[2,64,128]{2,1,0:T(8,128)S(1)}) custom-call(f32[4]{0:T(128)} %levels_hbm.1, s32[2,64,128]{2,1,0:T(8,128)} %labels_hbm.1, bf16[64,2,64,128]{3,2,1,0:T(8,128)(2,1)} %z_hbm.1, f32[2,64,128]{2,1,0:T(8,128)} %resid_hbm.1), custom_call_target="tpu_custom_call" | custom-call | tf_op jit(solution)/shard_map/deflated_coarse/pallas_call | solution.py:520
  39.1 0.7 %finish.1 = (f32[1,64]{1,0:T(1,128)}, f32[2,64,128]{2,1,0:T(8,128)}) custom-call(f32[1,64]{1,0:T(1,128)S(1)} %get-tuple-element.4.row, f32[2,64,128]{2,1,0:T(8,128)S(1)} %get-tuple-element.5.out), custom_call_target="tpu_custom_call" | custom-call | tf_op jit(solution)/shard_map/finish/pallas_call | solution.py:564

commit v8 on v7

--- a/solution.py
+++ b/solution.py
@@ -257,31 +257,40 @@
 
         return lax.fori_loop(0, modes // 8, some, jnp.zeros((8, depth), jnp.float32))
 
-    def expand_plane(plane):
+    def expand_part(plane, start, size):
         def some(block, acc):
             for inner in range(STEP):
                 k = block * STEP + inner
-                scale = jnp.broadcast_to(spread[pl.ds(k, 1), :], (height, depth))
-                acc = acc + zf[k, plane] * scale
+                scale = jnp.broadcast_to(spread[pl.ds(k, 1), :], (size, depth))
+                acc = acc + zf[k, plane, pl.ds(start, size)] * scale
             return acc
 
-        return lax.fori_loop(0, modes // STEP, some, jnp.zeros((height, depth), jnp.float32))
+        return lax.fori_loop(0, modes // STEP, some, jnp.zeros((size, depth), jnp.float32))
 
     def expand(which, row):
         spread_row(row)
         edges = edge_copies(which + 1)
-        sides_x = plane_copies(which + 1, field_send.at[which], field_x.at[which])
+        size = height // 2
+        sent = []
         for plane in range(planes):
-            value = expand_plane(plane)
-            field[which, plane] = value
-            field_send[which, plane] = value.astype(jnp.bfloat16)
-            if plane == 0:
-                sides_x[1].start()
-        sides_x[0].start()
+            for i in range(2):
+                span = pl.ds(i * size, size)
+                value = expand_part(plane, i * size, size)
+                field[which, plane, span] = value
+                field_send[which, plane, span] = value.astype(jnp.bfloat16)
+                mine = field_send.at[which, plane, span]
+                for side, target in enumerate((right, left)):
+                    if plane == (planes - 1 if side == 0 else 0):
+                        spot = (which + 1, 4 + 2 * side + i)
+                        copy = remote(mine, field_x.at[which, side, span], side_send.at[spot],
+                                      side_recv.at[spot], target)
+                        copy.start()
+                        sent.append(copy)
+        pending.extend(sent)
         edge_send[which + 1] = expand_edges()
         for copy in edges:
             copy.start()
-        return edges + sides_x
+        return edges + sent
 
     y_index = lax.broadcasted_iota(jnp.int32, (planes, height, depth), 1)
     z_index = lax.broadcasted_iota(jnp.int32, (planes, height, depth), 2)
@@ -546,8 +555,8 @@
             pltpu.VMEM((6,) + block, wide),
             pltpu.SMEM(levels.shape, wide),
             dma((3 + ZCHUNKS,)),
-            dma((3, 4)),
-            dma((3, 4)),
+            dma((3, 8)),
+            dma((3, 8)),
             dma((2,)),
             dma((2,)),
             dma((2,)),

time: 39.9 us -> 40.1 us (level)
  no operation moved by 1% of the time
where the time goes in v8:
time: 40.1 us; the launch traced here: 39.9 us
  Pallas kernels  39.3 us (98%)
  between operations  0.64 us (2%)
    pallas_call x1, Pallas kernels, body(): pl.pallas_call(functools.partial(kernel, sides), out_shape=(jax.ShapeDtyp...  38.6 us

profile of v8, /device:TPU:1, one launch (start us, length us, event | category | flops | bytes accessed | tf_op | source)
XLA Modules:
  0.0 39.9 jit_solution(17376383143834103840)
XLA Ops:
  0.6 38.6 %deflated_coarse.1 = (f32[1,64]{1,0:T(1,128)S(1)}, f32[2,64,128]{2,1,0:T(8,128)S(1)}) custom-call(f32[4]{0:T(128)} %levels_hbm.1, s32[2,64,128]{2,1,0:T(8,128)} %labels_hbm.1, bf16[64,2,64,128]{3,2,1,0:T(8,128)(2,1)} %z_hbm.1, f32[2,64,128]{2,1,0:T(8,128)} %resid_hbm.1), custom_call_target="tpu_custom_call" | custom-call | tf_op jit(solution)/shard_map/deflated_coarse/pallas_call | solution.py:529
  39.3 0.7 %finish.1 = (f32[1,64]{1,0:T(1,128)}, f32[2,64,128]{2,1,0:T(8,128)}) custom-call(f32[1,64]{1,0:T(1,128)S(1)} %get-tuple-element.4.row, f32[2,64,128]{2,1,0:T(8,128)S(1)} %get-tuple-element.5.out), custom_call_target="tpu_custom_call" | custom-call | tf_op jit(solution)/shard_map/finish/pallas_call | solution.py:573
